TPU v7x, 32 devices: a whole 2x2x4 slice. The times are simulated.
32 devices in a mesh: site: 8 (over z, y), mode: 4 (over x, core).
Axes of the slice: x: 2, y: 2, z: 4, core: 2. Of those that a mesh axis runs over, the one named last changes fastest.
Arguments:
- basis: bfloat16 [64, 400, 512], P('site', 'mode'), may hold values from -6 to 6
- images: bfloat16 [64, 400, 496], P('site', 'mode'), may hold values from -6 to 6
- hops: bfloat16 [64, 9, 400, 400], P('site', None, 'mode'), may hold values from -0.09375 to 0.09375
- neighbours: int32 [64, 8], P('site'), may hold values from 0 to 47, as said below
- rotation: bfloat16 [512, 512], replicated, may hold values from -0.25 to 0.25
Outputs:
- projected: float32 [512, 512], replicated
- rotated_basis: bfloat16 [64, 400, 512], P('site', 'mode')
- rotated_images: bfloat16 [64, 400, 512], P('site', 'mode')
Inputs may be any that keep to these rules, and one draw needn't show every extreme that they name: `neighbours`: the blocks form a periodic 4 x 4 x 4 x 64/64 lattice. Group s = 8 t + 4 gx + 2 gy + gz holds the 2 x 2 x 2 cube of time slice t at spatial offsets 2 gx, 2 gy, 2 gz, stored in its own order.
All inputs are finite; a program needn't handle non-finite values.
Results may differ from a plain program's by a relative error of at most 0.0026.
Values may be sent and summed in bfloat16 or wider, within the bound.
No kernel may reach another device: no remote copies, remote signals or barrier semaphores. Data moves between devices by JAX's collectives and lax.ppermute only.
A program may use at most 64 MiB of HBM per device.

v0:
```python
import math
import jax
import jax.numpy as jnp
from jax import lax
from jax.sharding import PartitionSpec as P

OLD = 496


def swapped(block, axis, distance):
    count = lax.axis_size(axis)
    route = []
    for low in range(count):
        high = low | 1 << distance
        if high != low and high < count:
            route += [(low, high), (high, low)]
    return lax.ppermute(block, axis, route)


def from_behind(block, axis, distance):
    devices = range(lax.axis_size(axis))
    route = [((i - distance) % len(devices), i) for i in devices]
    return lax.ppermute(block, axis, route)


def local(basis, images, hops, neighbours, rotation):
    local_blocks = basis.shape[0]
    modes_here = basis.shape[1]
    nvec = basis.shape[2]
    site_count = lax.axis_size("site")
    norm_scale = 1.0 / math.sqrt(site_count * local_blocks * modes_here * lax.axis_size("mode"))
    old_part = jnp.einsum("bci,bcj->ij", basis, images, preferred_element_type=jnp.float32)
    old_sum = lax.psum(old_part, ("site", "mode"))
    newest = jnp.transpose(basis[:, :, OLD:], (0, 2, 1))
    pieces = [newest]
    for bit in (2, 1, 0):
        pieces.append(swapped(newest, "site", bit))
    for offset in (-8, 8):
        if site_count > 8:
            pieces.append(from_behind(newest, "site", offset))
        else:
            pieces.append(newest)
    stacked = jnp.concatenate(pieces, axis=0)
    widened = lax.all_gather(stacked, "mode", axis=2, tiled=True)
    own_rows = jnp.arange(local_blocks, dtype=jnp.int32)
    row_index = jnp.concatenate([own_rows[:, None], neighbours], axis=1)
    gathered = widened[row_index]
    stencil = jnp.einsum("bdoi,bdki->bok", hops, gathered, preferred_element_type=jnp.float32)
    image_new = stencil.astype(jnp.bfloat16)
    images_all = jnp.concatenate([images, image_new], axis=2)
    new_part = jnp.einsum("bci,bck->ik", basis, image_new, preferred_element_type=jnp.float32)
    new_sum = lax.psum(new_part, ("site", "mode"))
    projected = jnp.concatenate([old_sum, new_sum], axis=1) * norm_scale
    flat_basis = basis.reshape(local_blocks * modes_here, nvec)
    flat_images = images_all.reshape(local_blocks * modes_here, nvec)
    rotated_basis = jnp.dot(flat_basis, rotation, preferred_element_type=jnp.float32).astype(
        jnp.bfloat16
    )
    rotated_images = jnp.dot(flat_images, rotation, preferred_element_type=jnp.float32).astype(
        jnp.bfloat16
    )
    return (
        projected,
        rotated_basis.reshape(local_blocks, modes_here, nvec),
        rotated_images.reshape(local_blocks, modes_here, nvec),
    )


def solution(mesh):
    placed = (
        P("site", "mode", None),
        P("site", "mode", None),
        P("site", None, "mode", None),
        P("site", None),
        P(),
    )
    return jax.shard_map(
        local,
        mesh=mesh,
        in_specs=placed,
        out_specs=(P(), P("site", "mode", None), P("site", "mode", None)),
        check_vma=False,
    )
```

profile of v0, /device:TPU:0, one launch (start us, length us, event | category | flops | bytes accessed | tf_op | source)
XLA Modules:
  0.0 156.1 jit_solution(4232743305024800474)
XLA Ops:
  7.2 1.1 slice.3
  8.3 0.2 copy.50
  8.5 4.1 %collective-permute-start = (bf16[8,16,100]{2,1,0:T(8,128)(2,1)S(1)}, bf16[8,16,100]{2,1,0:T(8,128)(2,1)S(1)}, u32[]{:S(2)}, u32[]{:S(2)}) collective-permute-start(bf16[8,16,100]{2,1,0:T(8,128)(2,1)S(1)} %bitcast.32), channel_id=1, source_target_pairs={{0,16},{16,0},{4,20},{20,4},{8,24},{24,8},{12,28},{28,12},{1,17},{... | collective-permute-start | bytes 76808 | tf_op jit(solution)/shard_map/ppermute | solution.py:17
  12.6 1.6 %collective-permute-start.1 = (bf16[8,16,100]{2,1,0:T(8,128)(2,1)S(1)}, bf16[8,16,100]{2,1,0:T(8,128)(2,1)S(1)}, u32[]{:S(2)}, u32[]{:S(2)}) collective-permute-start(bf16[8,16,100]{2,1,0:T(8,128)(2,1)S(1)} %bitcast.33), channel_id=1, source_target_pairs={{0,8},{8,0},{4,12},{12,4},{16,24},{24,16},{20,28},{28,20},{1,9},{9... | collective-permute-start | bytes 76808 | tf_op jit(solution)/shard_map/ppermute | solution.py:17
  14.2 1.5 collective-permute-start.2
  15.7 3.1 %convolution_bitcast_fusion = f32[512,496]{0,1:T(8,128)} fusion(bf16[8,100,512]{2,0,1:T(8,128)(2,1)} %param.5, bf16[8,100,496]{2,0,1:T(8,128)(2,1)} %param.6), kind=kOutput, calls=%fused_computation.5 | convolution fusion | flops 406323200 | bytes 2628608 | tf_op jit(solution)/shard_map/bci,bcj->ij/dot_general | solution.py:32
  18.9 0.2 copy.42
  19.1 0.4 copy-done.4
  19.8 0.6 convolution_convert_fusion.1
  20.6 1.1 copy.47
  21.8 0.4 copy.39
  22.3 14.5 %all_gather.3 = bf16[48,16,400]{0,1,2:T(8,128)(2,1)S(1)} all-gather(bf16[48,16,100]{0,1,2:T(8,128)(2,1)S(1)} %copy.39), channel_id=1, replica_groups=mesh['site'=8,'mode'=4] {'mode'}, dimensions={2}, use_global_device_ids=true | all-gather | bytes 768000 | tf_op jit(solution)/shard_map/all_gather | solution.py:44
  36.7 2.1 %copy.40 = bf16[48,16,400]{2,1,0:T(8,128)(2,1)S(1)} copy(bf16[48,16,400]{0,1,2:T(8,128)(2,1)S(1)} %all_gather.3) | data formatting | bytes 1228800 | tf_op jit(solution)/shard_map/all_gather | solution.py:44
  38.8 0.7 gather_fusion
  39.5 5.3 %fusion.8 = bf16[8,100,16]{1,2,0:T(8,128)(2,1)S(1)} fusion(bf16[8,9,16,400]{3,2,1,0:T(8,128)(2,1)S(1)} %bitcast.31, bf16[8,9,100,400]{3,0,2,1:T(8,128)(2,1)} %param.7), kind=kOutput, calls=%fused_computation.8 | convolution fusion | flops 92172800 | bytes 6707200 | tf_op jit(solution)/shard_map/bdoi,bdki->bok/dot_general | solution.py:48
  44.8 0.2 copy.44
  45.2 0.2 copy.45
  45.6 0.6 convolution_convert_fusion
  46.4 1.1 copy.48
  47.5 0.4 convolution_bitcast_fusion.1
  47.9 38.0 %psum.15 = f32[512,16]{0,1:T(8,128)S(1)} all-reduce(f32[512,16]{0,1:T(8,128)S(1)} %convolution_bitcast_fusion.1), channel_id=1, replica_groups=mesh['site'=8,'mode'=4] {'site','mode'}, use_global_device_ids=true, to_apply=%region_1.0 | all-reduce | flops 8192 | bytes 65536 | tf_op jit(solution)/shard_map/psum | solution.py:52
  85.9 60.7 %all-reduce.2.cloned.1.call-done = f32[512,496]{0,1:T(8,128)} async-done(((f32[512,496]{0,1:T(8,128)}), f32[512,496]{0,1:T(8,128)}) %all-reduce.2.cloned.1.call-update) | async-done | bytes 1015824 | tf_op jit(solution)/shard_map/psum | solution.py:33
  146.6 1.3 maximum_multiply_fusion
  147.9 1.3 copy.46
  (29 shorter events, 1.1 us)
Async XLA Ops:
  7.2 12.7 %copy-start = (bf16[512,512]{1,0:T(8,128)(2,1)S(1)}, bf16[512,512]{1,0:T(8,128)(2,1)}, u32[]{:S(2)}) copy-start(bf16[512,512]{1,0:T(8,128)(2,1)} %param.9) | copy-start | bytes 1572868
  7.2 139.4 %all-reduce.2.cloned.1.call-start = ((), (), s32[]{:S(2)}) async-start(), calls=%async_computation | async-start | bytes 2031616 | tf_op jit(solution)/shard_map/psum | solution.py:33
  8.5 10.3 %copy-start.1 = (bf16[8,100,512]{2,0,1:T(8,128)(2,1)S(1)}, bf16[8,100,512]{2,0,1:T(8,128)(2,1)}, u32[]{:S(2)}) copy-start(bf16[8,100,512]{2,0,1:T(8,128)(2,1)} %param.5) | copy-start | bytes 2457604
  8.5 13.2 %collective-permute-start = (bf16[8,16,100]{2,1,0:T(8,128)(2,1)S(1)}, bf16[8,16,100]{2,1,0:T(8,128)(2,1)S(1)}, u32[]{:S(2)}, u32[]{:S(2)}) collective-permute-start(bf16[8,16,100]{2,1,0:T(8,128)(2,1)S(1)} %bitcast.32), channel_id=1, source_target_pairs={{0,16},{16,0},{4,20},{20,4},{8,24},{24,8},{12,28},{28,12},{1,17},{... | collective-permute-start | bytes 76808 | tf_op jit(solution)/shard_map/ppermute | solution.py:17
  12.6 9.1 %collective-permute-start.1 = (bf16[8,16,100]{2,1,0:T(8,128)(2,1)S(1)}, bf16[8,16,100]{2,1,0:T(8,128)(2,1)S(1)}, u32[]{:S(2)}, u32[]{:S(2)}) collective-permute-start(bf16[8,16,100]{2,1,0:T(8,128)(2,1)S(1)} %bitcast.33), channel_id=1, source_target_pairs={{0,8},{8,0},{4,12},{12,4},{16,24},{24,16},{20,28},{28,20},{1,9},{9... | collective-permute-start | bytes 76808 | tf_op jit(solution)/shard_map/ppermute | solution.py:17
  14.2 7.5 %collective-permute-start.2 = (bf16[8,16,100]{2,1,0:T(8,128)(2,1)S(1)}, bf16[8,16,100]{2,1,0:T(8,128)(2,1)S(1)}, u32[]{:S(2)}, u32[]{:S(2)}) collective-permute-start(bf16[8,16,100]{2,1,0:T(8,128)(2,1)S(1)} %bitcast.34), channel_id=1, source_target_pairs={{0,4},{4,0},{8,12},{12,8},{16,20},{20,16},{24,28},{28,24},{1,5},{5... | collective-permute-start | bytes 76808 | tf_op jit(solution)/shard_map/ppermute | solution.py:17
  18.8 0.7 copy-start.4
  39.5 5.5 %copy-start.3 = (bf16[8,100,496]{2,0,1:T(8,128)(2,1)S(1)}, bf16[8,100,496]{2,0,1:T(8,128)(2,1)}, u32[]{:S(2)}) copy-start(bf16[8,100,496]{2,0,1:T(8,128)(2,1)} %param.6) | copy-start | bytes 2380804
  46.2 1.3 copy-start.2
Sparse Core Ops, SparseCore 0:
  19.0 127.5 all-reduce.1
where the time goes:
time: 156 us
  waiting for transfers between devices  60.7 us (39%)
  blocking collectives  52.5 us (34%)
  between operations  14.2 us (9%)
  matrix products  9.92 us (6%)
  local copies, waits for them, and re-layouts  9.89 us (6%)
  starting transfers between devices  7.26 us (5%)
  other arithmetic  1.57 us (1%)
    psum x1, waiting for transfers between devices, local(): old_sum = lax.psum(old_part, ('site', 'mode'))  60.7 us
    psum x1, blocking collectives, local(): new_sum = lax.psum(new_part, ('site', 'mode'))  38 us
    all_gather x1, blocking collectives, local(): widened = lax.all_gather(stacked, 'mode', axis=2, tiled=True)  14.5 us
    ppermute x3, starting transfers between devices, swapped(): return lax.ppermute(block, axis, route)  7.22 us
    dot_general x1, matrix products, local(): jnp.einsum('bdoi,bdki->bok', hops, gathered, preferred_element_type=jnp.f...  5.31 us
    unnamed x20, local copies, waits for them, and re-layouts  4.45 us
  transfers between devices with their start and end apart: 4, of which 1 were waited for; matrix products, arithmetic and copies ran while one was open for 11% of the time, Pallas kernels for 0%

commit v1 on v0

--- a/solution.py
+++ b/solution.py
@@ -3,6 +3,7 @@
 import jax.numpy as jnp
 from jax import lax
 from jax.sharding import PartitionSpec as P
+from jax.lax import all_gather
 
 OLD = 496
 
@@ -30,7 +31,7 @@
     site_count = lax.axis_size("site")
     norm_scale = 1.0 / math.sqrt(site_count * local_blocks * modes_here * lax.axis_size("mode"))
     old_part = jnp.einsum("bci,bcj->ij", basis, images, preferred_element_type=jnp.float32)
-    old_sum = lax.psum(old_part, ("site", "mode"))
+    old_sum = all_gather(old_part, axis_name=("site", "mode")).sum(axis=0)
     newest = jnp.transpose(basis[:, :, OLD:], (0, 2, 1))
     pieces = [newest]
     for bit in (2, 1, 0):

time: 156 us -> 258 us (1.65)
  waiting for transfers between devices: 60.7 us -> 116 us
  local copies, waits for them, and re-layouts: 9.89 us -> 43.1 us
  blocking collectives: 52.5 us -> 63.6 us
    all_gather x0 -> x1, waiting for transfers between devices: none -> 116 us  [local(): old_sum = all_gather(old_part, axis_name=('site', 'mode')).sum(axis=0)]
    psum x1 -> x0, waiting for transfers between devices: 60.7 us -> none  [local(): old_sum = lax.psum(old_part, ('site', 'mode'))]
    unnamed x20 -> x23, local copies, waits for them, and re-layouts: 4.45 us -> 38.7 us
    all_gather x1, blocking collectives: 14.5 us -> 21.4 us  [local(): widened = lax.all_gather(stacked, 'mode', axis=2, tiled=True)]
    psum x1, blocking collectives: 38 us -> 42.3 us  [local(): new_sum = lax.psum(new_part, ('site', 'mode'))]
    reduce_sum x0 -> x1, other arithmetic: none -> 3.08 us  [local(): old_sum = all_gather(old_part, axis_name=('site', 'mode')).sum(axis=0)]
  transfers between devices with their start and end apart: 4 -> 4, of which waited for: 1 -> 1; matrix products, arithmetic and copies ran while one was open for 11% -> 6% of each run, Pallas kernels for 0% -> 0%
where the time goes in v1:
time: 258 us
  waiting for transfers between devices  116 us (45%)
  blocking collectives  63.6 us (25%)
  local copies, waits for them, and re-layouts  43.1 us (17%)
  between operations  14.3 us (6%)
  matrix products  10 us (4%)
  starting transfers between devices  7.25 us (3%)
  other arithmetic  3.45 us (1%)
    all_gather x1, waiting for transfers between devices, local(): old_sum = all_gather(old_part, axis_name=('site', 'mode')).sum(axis=0)  116 us
    psum x1, blocking collectives, local(): new_sum = lax.psum(new_part, ('site', 'mode'))  42.3 us
    unnamed x23, local copies, waits for them, and re-layouts  38.7 us
    all_gather x1, blocking collectives, local(): widened = lax.all_gather(stacked, 'mode', axis=2, tiled=True)  21.4 us
    ppermute x3, starting transfers between devices, swapped(): return lax.ppermute(block, axis, route)  7.21 us
    dot_general x1, matrix products, local(): jnp.einsum('bdoi,bdki->bok', hops, gathered, preferred_element_type=jnp.f...  5.29 us
  transfers between devices with their start and end apart: 4, of which 1 were waited for; matrix products, arithmetic and copies ran while one was open for 6% of the time, Pallas kernels for 0%

profile of v1, /device:TPU:0, one launch (start us, length us, event | category | flops | bytes accessed | tf_op | source)
XLA Modules:
  0.0 257.5 jit_solution(11283658672276343849)
XLA Ops:
  7.2 3.2 %convolution_bitcast_fusion = f32[512,496]{0,1:T(8,128)} fusion(bf16[8,100,512]{2,0,1:T(8,128)(2,1)} %param.5, bf16[8,100,496]{2,0,1:T(8,128)(2,1)} %param.6), kind=kOutput, calls=%fused_computation.6 | convolution fusion | flops 406323200 | bytes 2628608 | tf_op jit(solution)/shard_map/bci,bcj->ij/dot_general | solution.py:33
  10.6 0.2 copy.50
  10.8 4.1 %collective-permute-start = (bf16[8,16,100]{2,1,0:T(8,128)(2,1)S(1)}, bf16[8,16,100]{2,1,0:T(8,128)(2,1)S(1)}, u32[]{:S(2)}, u32[]{:S(2)}) collective-permute-start(bf16[8,16,100]{2,1,0:T(8,128)(2,1)S(1)} %bitcast.38), channel_id=1, source_target_pairs={{0,16},{16,0},{4,20},{20,4},{8,24},{24,8},{12,28},{28,12},{1,17},{... | collective-permute-start | bytes 76808 | tf_op jit(solution)/shard_map/ppermute | solution.py:18
  14.9 1.6 collective-permute-start.1
  16.5 1.5 collective-permute-start.2
  18.0 0.2 copy.42
  18.6 0.6 convolution_convert_fusion.1
  19.3 1.1 copy.47
  20.6 0.4 copy.39
  21.0 21.4 %all_gather.11 = bf16[48,16,400]{0,1,2:T(8,128)(2,1)S(1)} all-gather(bf16[48,16,100]{0,1,2:T(8,128)(2,1)S(1)} %copy.39), channel_id=1, replica_groups=mesh['site'=8,'mode'=4] {'mode'}, dimensions={2}, use_global_device_ids=true | all-gather | bytes 768000 | tf_op jit(solution)/shard_map/all_gather | solution.py:45
  42.4 2.1 copy.40
  44.5 0.7 gather_fusion
  45.2 5.3 %fusion.8 = bf16[8,100,16]{1,2,0:T(8,128)(2,1)S(1)} fusion(bf16[8,9,16,400]{3,2,1,0:T(8,128)(2,1)S(1)} %bitcast.37, bf16[8,9,100,400]{3,0,2,1:T(8,128)(2,1)} %param.7), kind=kOutput, calls=%fused_computation.9 | convolution fusion | flops 92172800 | bytes 6707200 | tf_op jit(solution)/shard_map/bdoi,bdki->bok/dot_general | solution.py:49
  50.5 0.2 copy.44
  50.7 0.2 pad_maximum_fusion
  50.8 0.2 copy.45
  51.2 0.6 convolution_convert_fusion
  52.0 1.1 copy.48
  53.1 0.4 convolution_bitcast_fusion.1
  53.5 42.3 %psum.7 = f32[512,16]{0,1:T(8,128)S(1)} all-reduce(f32[512,16]{0,1:T(8,128)S(1)} %convolution_bitcast_fusion.1), channel_id=1, replica_groups=mesh['site'=8,'mode'=4] {'site','mode'}, use_global_device_ids=true, to_apply=%region_1.0 | all-reduce | flops 8192 | bytes 65536 | tf_op jit(solution)/shard_map/psum | solution.py:53
  95.8 115.8 %all-gather.3.cloned.1.call-done = f32[16384,496]{0,1:T(8,128)} async-done(((f32[512,496]{0,1:T(8,128)}), f32[16384,496]{0,1:T(8,128)}) %all-gather.3.cloned.1.call-update) | async-done | bytes 32505872 | tf_op jit(solution)/shard_map/all_gather | solution.py:34
  211.6 34.6 %copy.51 = f32[62,8,32,512]{3,2,1,0:T(8,128)S(1)} copy(f32[62,8,32,512]{3,1,2,0:T(8,128)} %bitcast.36) | data formatting | bytes 65011712
  246.2 3.1 %bitcast_reduce_fusion = f32[512,496]{0,1:T(8,128)S(1)} fusion(f32[62,8,32,512]{3,2,1,0:T(8,128)S(1)} %copy.51), kind=kLoop, calls=%fused_computation.1 | loop fusion | flops 7872512 | bytes 33521664 | tf_op jit(solution)/shard_map/reduce_sum | solution.py:34
  249.4 1.3 copy.46
  (33 shorter events, 1.1 us)
Async XLA Ops:
  7.2 11.4 %copy-start = (bf16[512,512]{1,0:T(8,128)(2,1)S(1)}, bf16[512,512]{1,0:T(8,128)(2,1)}, u32[]{:S(2)}) copy-start(bf16[512,512]{1,0:T(8,128)(2,1)} %param.9) | copy-start | bytes 1572868
  7.2 3.3 %copy-start.2 = (bf16[8,100,512]{2,0,1:T(8,128)(2,1)S(1)}, bf16[8,100,512]{2,0,1:T(8,128)(2,1)}, u32[]{:S(2)}) copy-start(bf16[8,100,512]{2,0,1:T(8,128)(2,1)} %param.5) | copy-start | bytes 2457604
  7.2 204.4 %all-gather.3.cloned.1.call-start = ((), (), s32[]{:S(2)}) async-start(), calls=%async_computation | async-start | bytes 33521664 | tf_op jit(solution)/shard_map/all_gather | solution.py:34
  10.4 7.8 %copy-start.5 = (s32[8,8]{1,0:T(8,128)S(1)}, s32[8,8]{1,0:T(8,128)}, u32[]{:S(2)}) copy-start(s32[8,8]{1,0:T(8,128)} %param.8) | copy-start | bytes 772
  10.8 9.7 %collective-permute-start = (bf16[8,16,100]{2,1,0:T(8,128)(2,1)S(1)}, bf16[8,16,100]{2,1,0:T(8,128)(2,1)S(1)}, u32[]{:S(2)}, u32[]{:S(2)}) collective-permute-start(bf16[8,16,100]{2,1,0:T(8,128)(2,1)S(1)} %bitcast.38), channel_id=1, source_target_pairs={{0,16},{16,0},{4,20},{20,4},{8,24},{24,8},{12,28},{28,12},{1,17},{... | collective-permute-start | bytes 76808 | tf_op jit(solution)/shard_map/ppermute | solution.py:18
  14.9 5.6 %collective-permute-start.1 = (bf16[8,16,100]{2,1,0:T(8,128)(2,1)S(1)}, bf16[8,16,100]{2,1,0:T(8,128)(2,1)S(1)}, u32[]{:S(2)}, u32[]{:S(2)}) collective-permute-start(bf16[8,16,100]{2,1,0:T(8,128)(2,1)S(1)} %bitcast.39), channel_id=1, source_target_pairs={{0,8},{8,0},{4,12},{12,4},{16,24},{24,16},{20,28},{28,20},{1,9},{9... | collective-permute-start | bytes 76808 | tf_op jit(solution)/shard_map/ppermute | solution.py:18
  16.5 4.1 %collective-permute-start.2 = (bf16[8,16,100]{2,1,0:T(8,128)(2,1)S(1)}, bf16[8,16,100]{2,1,0:T(8,128)(2,1)S(1)}, u32[]{:S(2)}, u32[]{:S(2)}) collective-permute-start(bf16[8,16,100]{2,1,0:T(8,128)(2,1)S(1)} %bitcast.40), channel_id=1, source_target_pairs={{0,4},{4,0},{8,12},{12,8},{16,20},{20,16},{24,28},{28,24},{1,5},{5... | collective-permute-start | bytes 76808 | tf_op jit(solution)/shard_map/ppermute | solution.py:18
  45.2 5.5 %copy-start.4 = (bf16[8,100,496]{2,0,1:T(8,128)(2,1)S(1)}, bf16[8,100,496]{2,0,1:T(8,128)(2,1)}, u32[]{:S(2)}) copy-start(bf16[8,100,496]{2,0,1:T(8,128)(2,1)} %param.6) | copy-start | bytes 2380804
  51.8 1.3 copy-start.3
  246.2 4.5 %copy-start.1 = (bf16[512,512]{1,0:T(8,128)(2,1)S(1)}, bf16[512,512]{1,0:T(8,128)(2,1)}, u32[]{:S(2)}) copy-start(bf16[512,512]{1,0:T(8,128)(2,1)} %param.9) | copy-start | bytes 1572868
Sparse Core Ops, SparseCore 0:
  11.5 200.0 all-gather.2
